TPU v7x, 32 devices: a whole 2x2x4 slice. The times are simulated.
32 devices in a mesh: item: 8 (over z, x), bucket: 4 (over y, core).
Axes of the slice: x: 2, y: 2, z: 4, core: 2. Of those that a mesh axis runs over, the one named last changes fastest.
Arguments:
- code_rows: bfloat16 [8192, 64], P('item'), may hold values from -6 to 6
- centroids: bfloat16 [32768, 64], P('bucket'), may hold values from -0.5 to 0.5
Outputs:
- grad_codes: float32 [8192, 64], P('item')
- new_centroids: float32 [32768, 64], P('bucket')
All inputs are finite; a program needn't handle non-finite values.
Results may differ from a plain program's by a relative error of at most 0.0032.
Values sent between devices are 32-bit elements; how exact they have to be, the bound alone decides.
No kernel may reach another device: no remote copies, remote signals or barrier semaphores. Data moves between devices by JAX's collectives and lax.ppermute only.
A program may use at most 128 MiB of HBM per device.

v0:
```python
import jax
import jax.numpy as jnp
from jax import lax
from jax.sharding import PartitionSpec as P

BUCKETS = 32768
ITERS = 3
score_scale = 20.0
step_rate = 0.2
epsilon = 1e-06


def joined(value, axis, join):
    pieces = jax.tree.map(lambda part: lax.all_gather(part, axis), value)
    head = jax.tree.map(lambda part: part[0], pieces)
    tail = jax.tree.map(lambda part: part[1:], pieces)
    so_far, _ = lax.scan(lambda so_far, piece: (join(so_far, piece), None), head, tail)
    return so_far


def scores_of(code_rows, centroids):
    return score_scale * lax.dot_general(
        code_rows, centroids, (((1,), (1,)), ((), ())), preferred_element_type=jnp.float32
    )


def lse_pair(first, second):
    highest = jnp.maximum(first[0], second[0])
    return (
        highest,
        first[1] * jnp.exp(first[0] - highest) + second[1] * jnp.exp(second[0] - highest),
    )


def stats_triple(first, second):
    highest = jnp.maximum(first[0], second[0])
    return (
        highest,
        first[1] * jnp.exp(first[0] - highest) + second[1] * jnp.exp(second[0] - highest),
        first[2] + second[2],
    )


def reduce_rows(values):
    highest = jnp.max(values, axis=1)
    summed = jnp.sum(jnp.exp(values - highest[:, None]), axis=1)
    highest, summed = joined((highest, summed), "bucket", lse_pair)
    return highest + jnp.log(summed)


def reduce_cols(values):
    highest = jnp.max(values, axis=0)
    summed = jnp.sum(jnp.exp(values - highest[None, :]), axis=0)
    highest, summed = joined((highest, summed), "item", lse_pair)
    return highest + jnp.log(summed)


def rescale(own_rows, gradient):
    moved = own_rows.astype(jnp.float32) - step_rate * gradient
    return moved * lax.rsqrt(jnp.mean(moved * moved, axis=1, keepdims=True) + epsilon)


def body(code_rows, centroids):
    rows_total = code_rows.shape[0] * lax.axis_size("item")
    log_rows = jnp.log(jnp.float32(rows_total))
    log_buckets = jnp.log(jnp.float32(BUCKETS))
    potential_col = jnp.zeros((centroids.shape[0],), jnp.float32)
    potential_row = jnp.zeros((code_rows.shape[0],), jnp.float32)
    for iteration in range(ITERS):
        potential_row = -log_rows - reduce_rows(
            scores_of(code_rows, centroids) + potential_col[None, :]
        )
        potential_col = -log_buckets - reduce_cols(
            scores_of(code_rows, centroids) + potential_row[:, None]
        )
    scores = scores_of(code_rows, centroids)
    plan = jnp.exp(scores + potential_row[:, None] + potential_col[None, :] + log_rows)
    masses = jnp.sum(plan, axis=1)
    highest = jnp.max(scores, axis=1)
    totals = jnp.sum(jnp.exp(scores - highest[:, None]), axis=1)
    highest, totals, masses = joined((highest, totals, masses), "bucket", stats_triple)
    delta = (masses[:, None] * jnp.exp(scores - highest[:, None]) / totals[:, None] - plan).astype(
        jnp.bfloat16
    )
    grad_codes = lax.psum(
        score_scale * jnp.dot(delta, centroids, preferred_element_type=jnp.float32), "bucket"
    )
    local_grad = score_scale * lax.dot_general(
        delta, code_rows, (((0,), (0,)), ((), ())), preferred_element_type=jnp.float32
    )
    gradient = lax.psum(local_grad, "item")
    new_centroids = rescale(centroids, gradient)
    return (grad_codes, new_centroids)


def solution(mesh):
    return jax.shard_map(
        body,
        mesh=mesh,
        in_specs=(P("item", None), P("bucket", None)),
        out_specs=(P("item", None), P("bucket", None)),
        check_vma=False,
    )
```

profile of v0, /device:TPU:0, one launch (start us, length us, event | category | flops | bytes accessed | tf_op | source)
XLA Modules:
  0.0 586.0 jit_solution(3918211216739394180)
XLA Ops:
  8.1 14.3 %fusion.2 = (f32[1024]{0:T(1024)S(1)}, f32[1024,8192]{1,0:T(8,128)}) fusion(bf16[1024,64]{0,1:T(8,128)(2,1)S(1)} %copy-done, bf16[8192,64]{0,1:T(8,128)(2,1)} %param.17), kind=kOutput, calls=%fused_computation.49 | convolution fusion | flops 1090518016 | bytes 34738176 | tf_op jit(solution)/shard_map/dot_general | solution.py:22
  22.4 6.2 %all-gather = f32[4096]{0:T(1024)S(1)} all-gather(f32[1024]{0:T(1024)S(1)} %get-tuple-element.326), channel_id=2, replica_groups=mesh['item'=8,'bucket'=4] {'bucket'}, dimensions={0}, use_global_device_ids=true | all-gather | bytes 20480 | tf_op jit(solution)/shard_map/all_gather | solution.py:14
  28.6 13.6 %exponential_reduce_fusion.5 = f32[1024]{0:T(1024)S(1)} fusion(f32[1024,8192]{1,0:T(8,128)} %get-tuple-element.327, f32[1024]{0:T(1024)S(1)} %get-tuple-element.326), kind=kLoop, calls=%fused_computation.29 | loop fusion | flops 16776192 | bytes 33562624 | tf_op jit(solution)/shard_map/reduce_sum | solution.py:80
  42.3 5.4 all-gather.1
  47.9 12.5 %add_reduce_fusion.3 = f32[8192]{0:T(1024)S(1)} fusion(f32[1024,8192]{1,0:T(8,128)} %get-tuple-element.327, f32[1024]{0:T(1024)S(1)} %add_subtract_fusion.5), kind=kLoop, calls=%fused_computation.33 | loop fusion | flops 16769024 | bytes 33591296 | tf_op jit(solution)/shard_map/reduce_max | solution.py:52
  60.4 14.0 %exponential_reduce_fusion.4 = f32[8192]{0:T(1024)S(1)} fusion(f32[1024,8192]{1,0:T(8,128)} %get-tuple-element.327, f32[8192]{0:T(1024)S(1)} %add_reduce_fusion.3, f32[1024]{0:T(1024)S(1)} %add_subtract_fusion.5), kind=kLoop, calls=%fused_computation.28 | loop fusion | flops 25157632 | bytes 33624064 | tf_op jit(solution)/shard_map/reduce_sum | solution.py:53
  74.4 31.4 %all-gather.2 = f32[65536]{0:T(1024)S(1)} all-gather(f32[8192]{0:T(1024)S(1)} %add_reduce_fusion.3), channel_id=4, replica_groups=mesh['item'=8,'bucket'=4] {'item'}, dimensions={0}, use_global_device_ids=true | all-gather | bytes 294912 | tf_op jit(solution)/shard_map/all_gather | solution.py:14
  105.8 30.7 %all-gather.3 = f32[65536]{0:T(1024)S(1)} all-gather(f32[8192]{0:T(1024)S(1)} %exponential_reduce_fusion.4), channel_id=5, replica_groups=mesh['item'=8,'bucket'=4] {'item'}, dimensions={0}, use_global_device_ids=true | all-gather | bytes 294912 | tf_op jit(solution)/shard_map/all_gather | solution.py:14
  137.6 12.2 %add_reduce_fusion.2 = f32[1024]{0:T(1024)S(1)} fusion(f32[1024,8192]{1,0:T(8,128)} %get-tuple-element.327, f32[8192]{0:T(1024)S(1)} %add_subtract_fusion.2), kind=kLoop, calls=%fused_computation.32 | loop fusion | flops 16776192 | bytes 33591296 | tf_op jit(solution)/shard_map/reduce_max | solution.py:45
  149.8 14.3 %exponential_reduce_fusion.3 = f32[1024]{0:T(1024)S(1)} fusion(f32[1024,8192]{1,0:T(8,128)} %get-tuple-element.327, f32[1024]{0:T(1024)S(1)} %add_reduce_fusion.2, f32[8192]{0:T(1024)S(1)} %add_subtract_fusion.2), kind=kLoop, calls=%fused_computation.27 | loop fusion | flops 25164800 | bytes 33595392 | tf_op jit(solution)/shard_map/reduce_sum | solution.py:46
  164.1 5.2 all-gather.4
  169.3 5.2 all-gather.5
  174.7 12.5 %add_reduce_fusion.1 = f32[8192]{0:T(1024)S(1)} fusion(f32[1024,8192]{1,0:T(8,128)} %get-tuple-element.327, f32[1024]{0:T(1024)S(1)} %add_subtract_fusion.4), kind=kLoop, calls=%fused_computation.31 | loop fusion | flops 16769024 | bytes 33591296 | tf_op jit(solution)/shard_map/reduce_max | solution.py:52
  187.2 14.0 %exponential_reduce_fusion.2 = f32[8192]{0:T(1024)S(1)} fusion(f32[1024,8192]{1,0:T(8,128)} %get-tuple-element.327, f32[8192]{0:T(1024)S(1)} %add_reduce_fusion.1, f32[1024]{0:T(1024)S(1)} %add_subtract_fusion.4), kind=kLoop, calls=%fused_computation.26 | loop fusion | flops 25157632 | bytes 33624064 | tf_op jit(solution)/shard_map/reduce_sum | solution.py:53
  201.2 30.9 %all-gather.6 = f32[65536]{0:T(1024)S(1)} all-gather(f32[8192]{0:T(1024)S(1)} %add_reduce_fusion.1), channel_id=8, replica_groups=mesh['item'=8,'bucket'=4] {'item'}, dimensions={0}, use_global_device_ids=true | all-gather | bytes 294912 | tf_op jit(solution)/shard_map/all_gather | solution.py:14
  232.1 30.7 %all-gather.7 = f32[65536]{0:T(1024)S(1)} all-gather(f32[8192]{0:T(1024)S(1)} %exponential_reduce_fusion.2), channel_id=9, replica_groups=mesh['item'=8,'bucket'=4] {'item'}, dimensions={0}, use_global_device_ids=true | all-gather | bytes 294912 | tf_op jit(solution)/shard_map/all_gather | solution.py:14
  263.9 12.2 %add_reduce_fusion = f32[1024]{0:T(1024)S(1)} fusion(f32[1024,8192]{1,0:T(8,128)} %get-tuple-element.327, f32[8192]{0:T(1024)S(1)} %add_subtract_fusion.1), kind=kLoop, calls=%fused_computation.30 | loop fusion | flops 16776192 | bytes 33591296 | tf_op jit(solution)/shard_map/reduce_max | solution.py:45
  276.1 14.3 %exponential_reduce_fusion.1 = f32[1024]{0:T(1024)S(1)} fusion(f32[1024,8192]{1,0:T(8,128)} %get-tuple-element.327, f32[1024]{0:T(1024)S(1)} %add_reduce_fusion, f32[8192]{0:T(1024)S(1)} %add_subtract_fusion.1), kind=kLoop, calls=%fused_computation.25 | loop fusion | flops 25164800 | bytes 33595392 | tf_op jit(solution)/shard_map/reduce_sum | solution.py:46
  290.4 5.2 all-gather.8
  295.6 5.4 all-gather.9
  301.2 12.5 %add_reduce_fusion.4 = f32[8192]{0:T(1024)S(1)} fusion(f32[1024,8192]{1,0:T(8,128)} %get-tuple-element.327, f32[1024]{0:T(1024)S(1)} %add_subtract_fusion.3), kind=kLoop, calls=%fused_computation.34 | loop fusion | flops 16769024 | bytes 33591296 | tf_op jit(solution)/shard_map/reduce_max | solution.py:52
  313.7 14.0 %exponential_reduce_fusion = f32[8192]{0:T(1024)S(1)} fusion(f32[1024,8192]{1,0:T(8,128)} %get-tuple-element.327, f32[8192]{0:T(1024)S(1)} %add_reduce_fusion.4, f32[1024]{0:T(1024)S(1)} %add_subtract_fusion.3), kind=kLoop, calls=%fused_computation.24 | loop fusion | flops 25157632 | bytes 33624064 | tf_op jit(solution)/shard_map/reduce_sum | solution.py:53
  327.7 30.9 %all-gather.10 = f32[65536]{0:T(1024)S(1)} all-gather(f32[8192]{0:T(1024)S(1)} %add_reduce_fusion.4), channel_id=12, replica_groups=mesh['item'=8,'bucket'=4] {'item'}, dimensions={0}, use_global_device_ids=true | all-gather | bytes 294912 | tf_op jit(solution)/shard_map/all_gather | solution.py:14
  358.6 30.7 %all-gather.11 = f32[65536]{0:T(1024)S(1)} all-gather(f32[8192]{0:T(1024)S(1)} %exponential_reduce_fusion), channel_id=13, replica_groups=mesh['item'=8,'bucket'=4] {'item'}, dimensions={0}, use_global_device_ids=true | all-gather | bytes 294912 | tf_op jit(solution)/shard_map/all_gather | solution.py:14
  390.4 14.8 %fusion = f32[1024]{0:T(1024)S(1)} fusion(f32[1024,8192]{1,0:T(8,128)} %get-tuple-element.327, f32[8192]{0:T(1024)S(1)} %add_subtract_fusion, f32[1024]{0:T(1024)S(1)} %add_subtract_fusion.3), kind=kLoop, calls=%fused_computation.35 | loop fusion | flops 33553408 | bytes 33595392 | tf_op jit(solution)/shard_map/reduce_sum | solution.py:78
  405.2 5.2 all-gather.12
  410.7 18.8 %subtract_convert_fusion = bf16[1024,8192]{1,0:T(8,128)(2,1)S(1)} fusion(f32[1024,8192]{1,0:T(8,128)} %get-tuple-element.327, f32[1024]{0:T(1024)S(1)} %get-tuple-element.223, f32[1024]{0:T(1024)S(1)} %get-tuple-element.222, f32[1024]{0:T(1024)S(1)} %get-tuple-element.221, f32[8192]{0:T(1024)S(1)} %add_subtract_fusion, f32[1024]{0:T(1024)S(1)} %add_subtract_fusion.3), kind=kLoop, calls=%fused_computation.22 | loop fusion | flops 67108864 | bytes 50380800 | tf_op jit(solution)/shard_map/convert_element_type | solution.py:82
  429.5 5.7 copy-done.1
  435.2 4.3 convolution_multiply_fusion
  439.8 11.7 %convolution_multiply_fusion.1 = f32[1024,64]{0,1:T(8,128)} fusion(bf16[1024,8192]{1,0:T(8,128)(2,1)} %copy-done.1, bf16[8192,64]{0,1:T(8,128)(2,1)S(1)} %copy-done.2), kind=kOutput, calls=%fused_computation.41 | convolution fusion | flops 1073807360 | bytes 18087936 | tf_op jit(solution)/shard_map/dot_general | solution.py:86
  451.5 91.4 %all-reduce.5.cloned.1.call-done = f32[8192,64]{0,1:T(8,128)} async-done(((f32[8192,64]{0,1:T(8,128)}), f32[8192,64]{0,1:T(8,128)}) %all-reduce.5.cloned.1.call-update) | async-done | bytes 2097168 | tf_op jit(solution)/shard_map/psum | solution.py:91
  548.2 29.2 %all-reduce.3.cloned.1.call-done = f32[1024,64]{0,1:T(8,128)} async-done(((f32[1024,64]{0,1:T(8,128)}), f32[1024,64]{0,1:T(8,128)}) %all-reduce.3.cloned.1.call-update) | async-done | bytes 262160 | tf_op jit(solution)/shard_map/psum | solution.py:85
  (139 shorter events, 14.7 us)
Async XLA Ops:
  7.2 0.9 copy-start
  7.2 535.8 %all-reduce.5.cloned.1.call-start = ((), (), s32[]{:S(2)}) async-start(), calls=%async_computation.1 | async-start | bytes 4194304 | tf_op jit(solution)/shard_map/psum | solution.py:91
  410.6 29.2 %copy-start.2 = (bf16[8192,64]{0,1:T(8,128)(2,1)S(1)}, bf16[8192,64]{0,1:T(8,128)(2,1)}, u32[]{:S(2)}) copy-start(bf16[8192,64]{0,1:T(8,128)(2,1)} %param.17) | copy-start | bytes 3145732
  429.5 5.7 copy-start.1
  439.5 137.9 %all-reduce.3.cloned.1.call-start = ((), (), s32[]{:S(2)}) async-start(), calls=%async_computation | async-start | bytes 524288 | tf_op jit(solution)/shard_map/psum | solution.py:85
Sparse Core Ops, SparseCore 0:
  439.7 103.2 all-reduce.4
  545.9 31.5 all-reduce.2
where the time goes:
time: 588 us; the launch traced here: 586 us
  blocking collectives  223 us (38%)
  other arithmetic  186 us (32%)
  waiting for transfers between devices  121 us (21%)
  matrix products  30.3 us (5%)
  between operations  14.4 us (2%)
  local copies, waits for them, and re-layouts  10.4 us (2%)
    all_gather x13, blocking collectives, joined(): pieces = jax.tree.map(lambda part: lax.all_gather(part, axis), value)  223 us
    psum x1, waiting for transfers between devices, body(): gradient = lax.psum(local_grad, 'item')  91.4 us
    reduce_sum x3, other arithmetic, reduce_cols(): summed = jnp.sum(jnp.exp(values - highest[None, :]), axis=0)  41.9 us
    reduce_max x3, other arithmetic, reduce_cols(): highest = jnp.max(values, axis=0)  37.4 us
    psum x1, waiting for transfers between devices, body(): lax.psum(score_scale * jnp.dot(delta, centroids, preferred_element_type=j...  29.2 us
    reduce_sum x2, other arithmetic, reduce_rows(): summed = jnp.sum(jnp.exp(values - highest[:, None]), axis=1)  28.6 us
    reduce_max x2, other arithmetic, reduce_rows(): highest = jnp.max(values, axis=1)  24.3 us
    convert_element_type x1, other arithmetic, body(): (masses[:, None] * jnp.exp(scores - highest[:, None]) / totals[:, None] -...  18.8 us
  transfers between devices with their start and end apart: 2, of which 2 were waited for; matrix products, arithmetic and copies ran while one was open for 3% of the time, Pallas kernels for 0%

commit v1 on v0

--- a/solution.py
+++ b/solution.py
@@ -82,7 +82,10 @@
     delta = (masses[:, None] * jnp.exp(scores - highest[:, None]) / totals[:, None] - plan).astype(
         jnp.bfloat16
     )
-    grad_codes = lax.psum(
+    _mark_classes = lambda in_array, axis_key: jnp.sum(
+        jax.lax.all_gather(in_array, axis_name=axis_key), axis=0
+    )
+    grad_codes = _mark_classes(
         score_scale * jnp.dot(delta, centroids, preferred_element_type=jnp.float32), "bucket"
     )
     local_grad = score_scale * lax.dot_general(

time: 588 us -> 569 us (0.968)
  waiting for transfers between devices: 121 us -> 99.7 us
    psum x1 -> x0, waiting for transfers between devices: 29.2 us -> none  [body(): lax.psum(score_scale * jnp.dot(delta, centroids, preferred_element_type=j...]
    all_gather x0 -> x1, waiting for transfers between devices: none -> 7.38 us  [body(): jax.lax.all_gather(in_array, axis_name=axis_key)]
  transfers between devices with their start and end apart: 2 -> 2, of which waited for: 2 -> 2; matrix products, arithmetic and copies ran while one was open for 3% -> 2% of each run, Pallas kernels for 0% -> 0%
where the time goes in v1:
time: 569 us; the launch traced here: 568 us
  blocking collectives  223 us (39%)
  other arithmetic  187 us (33%)
  waiting for transfers between devices  99.7 us (18%)
  matrix products  30.3 us (5%)
  between operations  15.8 us (3%)
  local copies, waits for them, and re-layouts  10.6 us (2%)
    all_gather x13, blocking collectives, joined(): pieces = jax.tree.map(lambda part: lax.all_gather(part, axis), value)  223 us
    psum x1, waiting for transfers between devices, body(): gradient = lax.psum(local_grad, 'item')  92.3 us
    reduce_sum x3, other arithmetic, reduce_cols(): summed = jnp.sum(jnp.exp(values - highest[None, :]), axis=0)  41.9 us
    reduce_max x3, other arithmetic, reduce_cols(): highest = jnp.max(values, axis=0)  37.4 us
    reduce_sum x2, other arithmetic, reduce_rows(): summed = jnp.sum(jnp.exp(values - highest[:, None]), axis=1)  28.6 us
    reduce_max x2, other arithmetic, reduce_rows(): highest = jnp.max(values, axis=1)  24.4 us
    convert_element_type x1, other arithmetic, body(): (masses[:, None] * jnp.exp(scores - highest[:, None]) / totals[:, None] -...  18.7 us
    reduce_sum x1, other arithmetic, body(): masses = jnp.sum(plan, axis=1)  14.6 us
  transfers between devices with their start and end apart: 2, of which 2 were waited for; matrix products, arithmetic and copies ran while one was open for 2% of the time, Pallas kernels for 0%

profile of v1, /device:TPU:0, one launch (start us, length us, event | category | flops | bytes accessed | tf_op | source)
XLA Modules:
  0.0 567.8 jit_solution(10975580398263308968)
XLA Ops:
  8.9 14.3 %fusion.2 = (f32[1024]{0:T(1024)S(1)}, f32[1024,8192]{1,0:T(8,128)}) fusion(bf16[1024,64]{0,1:T(8,128)(2,1)S(1)} %copy-done, bf16[8192,64]{0,1:T(8,128)(2,1)} %param.17), kind=kOutput, calls=%fused_computation.49 | convolution fusion | flops 1090518016 | bytes 34738176 | tf_op jit(solution)/shard_map/dot_general | solution.py:22
  23.2 6.3 %all-gather = f32[4096]{0:T(1024)S(1)} all-gather(f32[1024]{0:T(1024)S(1)} %get-tuple-element.326), channel_id=2, replica_groups=mesh['item'=8,'bucket'=4] {'bucket'}, dimensions={0}, use_global_device_ids=true | all-gather | bytes 20480 | tf_op jit(solution)/shard_map/all_gather | solution.py:14
  29.5 13.6 %exponential_reduce_fusion.5 = f32[1024]{0:T(1024)S(1)} fusion(f32[1024,8192]{1,0:T(8,128)} %get-tuple-element.327, f32[1024]{0:T(1024)S(1)} %get-tuple-element.326), kind=kLoop, calls=%fused_computation.29 | loop fusion | flops 16776192 | bytes 33562624 | tf_op jit(solution)/shard_map/reduce_sum | solution.py:80
  43.1 5.4 all-gather.1
  48.8 12.5 %add_reduce_fusion.3 = f32[8192]{0:T(1024)S(1)} fusion(f32[1024,8192]{1,0:T(8,128)} %get-tuple-element.327, f32[1024]{0:T(1024)S(1)} %add_subtract_fusion.5), kind=kLoop, calls=%fused_computation.33 | loop fusion | flops 16769024 | bytes 33591296 | tf_op jit(solution)/shard_map/reduce_max | solution.py:52
  61.2 14.0 %exponential_reduce_fusion.4 = f32[8192]{0:T(1024)S(1)} fusion(f32[1024,8192]{1,0:T(8,128)} %get-tuple-element.327, f32[8192]{0:T(1024)S(1)} %add_reduce_fusion.3, f32[1024]{0:T(1024)S(1)} %add_subtract_fusion.5), kind=kLoop, calls=%fused_computation.28 | loop fusion | flops 25157632 | bytes 33624064 | tf_op jit(solution)/shard_map/reduce_sum | solution.py:53
  75.2 31.4 %all-gather.2 = f32[65536]{0:T(1024)S(1)} all-gather(f32[8192]{0:T(1024)S(1)} %add_reduce_fusion.3), channel_id=4, replica_groups=mesh['item'=8,'bucket'=4] {'item'}, dimensions={0}, use_global_device_ids=true | all-gather | bytes 294912 | tf_op jit(solution)/shard_map/all_gather | solution.py:14
  106.6 30.7 %all-gather.3 = f32[65536]{0:T(1024)S(1)} all-gather(f32[8192]{0:T(1024)S(1)} %exponential_reduce_fusion.4), channel_id=5, replica_groups=mesh['item'=8,'bucket'=4] {'item'}, dimensions={0}, use_global_device_ids=true | all-gather | bytes 294912 | tf_op jit(solution)/shard_map/all_gather | solution.py:14
  138.5 12.2 %add_reduce_fusion.2 = f32[1024]{0:T(1024)S(1)} fusion(f32[1024,8192]{1,0:T(8,128)} %get-tuple-element.327, f32[8192]{0:T(1024)S(1)} %add_subtract_fusion.2), kind=kLoop, calls=%fused_computation.32 | loop fusion | flops 16776192 | bytes 33591296 | tf_op jit(solution)/shard_map/reduce_max | solution.py:45
  150.7 14.3 %exponential_reduce_fusion.3 = f32[1024]{0:T(1024)S(1)} fusion(f32[1024,8192]{1,0:T(8,128)} %get-tuple-element.327, f32[1024]{0:T(1024)S(1)} %add_reduce_fusion.2, f32[8192]{0:T(1024)S(1)} %add_subtract_fusion.2), kind=kLoop, calls=%fused_computation.27 | loop fusion | flops 25164800 | bytes 33595392 | tf_op jit(solution)/shard_map/reduce_sum | solution.py:46
  165.0 5.2 all-gather.4
  170.2 5.2 all-gather.5
  175.6 12.5 %add_reduce_fusion.1 = f32[8192]{0:T(1024)S(1)} fusion(f32[1024,8192]{1,0:T(8,128)} %get-tuple-element.327, f32[1024]{0:T(1024)S(1)} %add_subtract_fusion.4), kind=kLoop, calls=%fused_computation.31 | loop fusion | flops 16769024 | bytes 33591296 | tf_op jit(solution)/shard_map/reduce_max | solution.py:52
  188.0 14.0 %exponential_reduce_fusion.2 = f32[8192]{0:T(1024)S(1)} fusion(f32[1024,8192]{1,0:T(8,128)} %get-tuple-element.327, f32[8192]{0:T(1024)S(1)} %add_reduce_fusion.1, f32[1024]{0:T(1024)S(1)} %add_subtract_fusion.4), kind=kLoop, calls=%fused_computation.26 | loop fusion | flops 25157632 | bytes 33624064 | tf_op jit(solution)/shard_map/reduce_sum | solution.py:53
  202.0 30.9 %all-gather.6 = f32[65536]{0:T(1024)S(1)} all-gather(f32[8192]{0:T(1024)S(1)} %add_reduce_fusion.1), channel_id=8, replica_groups=mesh['item'=8,'bucket'=4] {'item'}, dimensions={0}, use_global_device_ids=true | all-gather | bytes 294912 | tf_op jit(solution)/shard_map/all_gather | solution.py:14
  232.9 30.7 %all-gather.7 = f32[65536]{0:T(1024)S(1)} all-gather(f32[8192]{0:T(1024)S(1)} %exponential_reduce_fusion.2), channel_id=9, replica_groups=mesh['item'=8,'bucket'=4] {'item'}, dimensions={0}, use_global_device_ids=true | all-gather | bytes 294912 | tf_op jit(solution)/shard_map/all_gather | solution.py:14
  264.7 12.2 %add_reduce_fusion = f32[1024]{0:T(1024)S(1)} fusion(f32[1024,8192]{1,0:T(8,128)} %get-tuple-element.327, f32[8192]{0:T(1024)S(1)} %add_subtract_fusion.1), kind=kLoop, calls=%fused_computation.30 | loop fusion | flops 16776192 | bytes 33591296 | tf_op jit(solution)/shard_map/reduce_max | solution.py:45
  276.9 14.3 %exponential_reduce_fusion.1 = f32[1024]{0:T(1024)S(1)} fusion(f32[1024,8192]{1,0:T(8,128)} %get-tuple-element.327, f32[1024]{0:T(1024)S(1)} %add_reduce_fusion, f32[8192]{0:T(1024)S(1)} %add_subtract_fusion.1), kind=kLoop, calls=%fused_computation.25 | loop fusion | flops 25164800 | bytes 33595392 | tf_op jit(solution)/shard_map/reduce_sum | solution.py:46
  291.2 5.2 all-gather.8
  296.5 5.4 all-gather.9
  302.0 12.5 %add_reduce_fusion.4 = f32[8192]{0:T(1024)S(1)} fusion(f32[1024,8192]{1,0:T(8,128)} %get-tuple-element.327, f32[1024]{0:T(1024)S(1)} %add_subtract_fusion.3), kind=kLoop, calls=%fused_computation.34 | loop fusion | flops 16769024 | bytes 33591296 | tf_op jit(solution)/shard_map/reduce_max | solution.py:52
  314.5 14.0 %exponential_reduce_fusion = f32[8192]{0:T(1024)S(1)} fusion(f32[1024,8192]{1,0:T(8,128)} %get-tuple-element.327, f32[8192]{0:T(1024)S(1)} %add_reduce_fusion.4, f32[1024]{0:T(1024)S(1)} %add_subtract_fusion.3), kind=kLoop, calls=%fused_computation.24 | loop fusion | flops 25157632 | bytes 33624064 | tf_op jit(solution)/shard_map/reduce_sum | solution.py:53
  328.5 30.9 %all-gather.10 = f32[65536]{0:T(1024)S(1)} all-gather(f32[8192]{0:T(1024)S(1)} %add_reduce_fusion.4), channel_id=12, replica_groups=mesh['item'=8,'bucket'=4] {'item'}, dimensions={0}, use_global_device_ids=true | all-gather | bytes 294912 | tf_op jit(solution)/shard_map/all_gather | solution.py:14
  359.4 30.7 %all-gather.11 = f32[65536]{0:T(1024)S(1)} all-gather(f32[8192]{0:T(1024)S(1)} %exponential_reduce_fusion), channel_id=13, replica_groups=mesh['item'=8,'bucket'=4] {'item'}, dimensions={0}, use_global_device_ids=true | all-gather | bytes 294912 | tf_op jit(solution)/shard_map/all_gather | solution.py:14
  391.2 14.6 %fusion = f32[1024]{0:T(1024)S(1)} fusion(f32[1024,8192]{1,0:T(8,128)} %get-tuple-element.327, f32[8192]{0:T(1024)S(1)} %add_subtract_fusion, f32[1024]{0:T(1024)S(1)} %add_subtract_fusion.3), kind=kLoop, calls=%fused_computation.35 | loop fusion | flops 33553408 | bytes 33595392 | tf_op jit(solution)/shard_map/reduce_sum | solution.py:78
  405.8 5.3 all-gather.12
  411.4 18.7 %subtract_convert_fusion = bf16[1024,8192]{1,0:T(8,128)(2,1)S(1)} fusion(f32[1024,8192]{1,0:T(8,128)} %get-tuple-element.327, f32[1024]{0:T(1024)S(1)} %get-tuple-element.223, f32[1024]{0:T(1024)S(1)} %get-tuple-element.222, f32[1024]{0:T(1024)S(1)} %get-tuple-element.221, f32[8192]{0:T(1024)S(1)} %add_subtract_fusion, f32[1024]{0:T(1024)S(1)} %add_subtract_fusion.3), kind=kLoop, calls=%fused_computation.22 | loop fusion | flops 67108864 | bytes 50380800 | tf_op jit(solution)/shard_map/convert_element_type | solution.py:82
  430.1 5.7 %copy-done.1 = bf16[1024,8192]{1,0:T(8,128)(2,1)} copy-done((bf16[1024,8192]{1,0:T(8,128)(2,1)}, bf16[1024,8192]{1,0:T(8,128)(2,1)S(1)}, u32[]{:S(2)}) %copy-start.1) | copy-done | bytes 16777240
  435.8 5.9 %convolution_multiply_fusion.1 = f32[1024,64]{0,1:T(8,128)} fusion(bf16[1024,8192]{1,0:T(8,128)(2,1)S(1)} %subtract_convert_fusion, bf16[8192,64]{0,1:T(8,128)(2,1)S(1)} %copy-done.2), kind=kOutput, calls=%fused_computation.41 | convolution fusion | flops 1073807360 | bytes 18087936 | tf_op jit(solution)/shard_map/dot_general | solution.py:89
  442.1 10.1 %convolution_multiply_fusion = f32[8192,64]{0,1:T(8,128)} fusion(bf16[1024,64]{0,1:T(8,128)(2,1)S(1)} %copy-done, bf16[1024,8192]{1,0:T(8,128)(2,1)} %copy-done.1), kind=kOutput, calls=%fused_computation.37 | convolution fusion | flops 1074266112 | bytes 19005440 | tf_op jit(solution)/shard_map/dot_general | solution.py:91
  452.2 7.4 %all-gather.16.cloned.1.call-done = f32[4096,64]{0,1:T(8,128)} async-done(((f32[1024,64]{0,1:T(8,128)}), f32[4096,64]{0,1:T(8,128)}) %all-gather.16.cloned.1.call-update) | async-done | bytes 1048592 | tf_op jit(solution)/shard_map/all_gather | solution.py:86
  462.9 92.3 %all-reduce.2.cloned.1.call-done = f32[8192,64]{0,1:T(8,128)} async-done(((f32[8192,64]{0,1:T(8,128)}), f32[8192,64]{0,1:T(8,128)}) %all-reduce.2.cloned.1.call-update) | async-done | bytes 2097168 | tf_op jit(solution)/shard_map/psum | solution.py:94
  (140 shorter events, 16.3 us)
Async XLA Ops:
  8.0 0.9 copy-start
  8.0 451.6 %all-gather.16.cloned.1.call-start = ((), (), s32[]{:S(2)}) async-start(), calls=%async_computation.1 | async-start | bytes 1310720 | tf_op jit(solution)/shard_map/all_gather | solution.py:86
  405.8 30.0 %copy-start.2 = (bf16[8192,64]{0,1:T(8,128)(2,1)S(1)}, bf16[8192,64]{0,1:T(8,128)(2,1)}, u32[]{:S(2)}) copy-start(bf16[8192,64]{0,1:T(8,128)(2,1)} %param.17) | copy-start | bytes 3145732
  430.1 5.7 %copy-start.1 = (bf16[1024,8192]{1,0:T(8,128)(2,1)}, bf16[1024,8192]{1,0:T(8,128)(2,1)S(1)}, u32[]{:S(2)}) copy-start(bf16[1024,8192]{1,0:T(8,128)(2,1)S(1)} %subtract_convert_fusion) | copy-start | bytes 50331652
  441.8 113.4 %all-reduce.2.cloned.1.call-start = ((), (), s32[]{:S(2)}) async-start(), calls=%async_computation | async-start | bytes 4194304 | tf_op jit(solution)/shard_map/psum | solution.py:94
Sparse Core Ops, SparseCore 0:
  441.9 17.6 all-gather.15
Sparse Core Ops, SparseCore 1:
  452.3 102.8 all-reduce.1
